TPU v7x, 1024 devices: a whole 4x4x32 slice. The times are simulated.
1024 devices in a mesh: wide: 32 (over x, z_lo), narrow: 32 (over y, z_hi, core).
Axes of the slice: x: 4, y: 4, z: 32 (z_hi: 4, z_lo: 8; z = z_hi * 8 + z_lo), core: 2. Of those that a mesh axis runs over, the one named last changes fastest.
Arguments:
- state: float32 [32, 512, 512], P('narrow'), may hold values from -1.5 to 1.5
- left_env: float32 [32, 32, 512, 512], P('wide', 'narrow')
- right_env: float32 [32, 32, 512, 512], P('wide', 'narrow')
- left_sizes: int32 [32], replicated, may hold values from 1 to 512, 12288 in all
- right_sizes: int32 [32], replicated, may hold values from 1 to 512, 12288 in all
- channel_charge: int32 [32], P('wide'), may hold values from 0 to 2
Outputs:
- lanczos_vector: float32 [32, 512, 512], P('narrow', 'wide')
- alpha: float32 [], replicated
Inputs may be any that keep to these rules, and one draw needn't show every extreme that they name: `left_sizes`: basis states of each left sector; they add up to 12288, and some sector has exactly 512. `right_sizes`: basis states of each right sector; they add up to 12288, and some sector has exactly 512. `channel_charge`: 0 lowers the sector by one, 1 keeps it, 2 raises it by one.
All inputs are finite; a program needn't handle non-finite values.
Results may differ from a plain program's by a relative error of at most 0.0003.
Values sent between devices are 32-bit elements; how exact they have to be, the bound alone decides.
A program may use at most 32 MiB of HBM per device.

v0:
```python
import jax
import jax.numpy as jnp
from jax import lax
from jax.sharding import PartitionSpec as P


def with_halo(cells, sides, width):
    for axis, dim in sides:
        count = lax.axis_size(axis)
        ends = count - 1
        head = lax.slice_in_dim(cells, 0, width, axis=dim)
        tail = lax.slice_in_dim(cells, cells.shape[dim] - width, cells.shape[dim], axis=dim)
        cells = jnp.concatenate(
            [
                lax.ppermute(tail, axis, [(i, (i + 1) % count) for i in range(ends)]),
                cells,
                lax.ppermute(head, axis, [((i + 1) % count, i) for i in range(ends)]),
            ],
            axis=dim,
        )
    return cells


def valid_vector(sizes, sector, block):
    labels = jnp.arange(sizes.shape[0], dtype=jnp.int32)
    count = jnp.sum(jnp.where(labels == sector, sizes, 0))
    positions = jnp.arange(block, dtype=jnp.int32)
    return (positions < count).astype(jnp.float32)


def per_device(state, left_env, right_env, left_sizes, right_sizes, channel_charge):
    sec_local = state.shape[0]
    block = state.shape[1]
    n_wide = lax.axis_size("wide")
    band = block // n_wide
    narrow_pos = lax.axis_index("narrow")
    wide_pos = lax.axis_index("wide")
    first = narrow_pos * sec_local
    sec = 0
    rows_ok = valid_vector(left_sizes, first + sec, block)
    cols_ok = valid_vector(right_sizes, first + sec, block)
    own_masks = [state[sec] * rows_ok[:, None] * cols_ok[None, :]]
    psi = jnp.stack(own_masks)
    chan = 0
    shift_by = channel_charge[chan] - 1
    sec = 0
    sector = first + sec
    source = sector - shift_by
    lmat = (
        left_env[chan, sec]
        * valid_vector(left_sizes, sector, block)[:, None]
        * valid_vector(left_sizes, source, block)[None, :]
    )
    rmat = (
        right_env[chan, sec]
        * valid_vector(right_sizes, sector, block)[:, None]
        * valid_vector(right_sizes, source, block)[None, :]
    )
    lmats = [lmat]
    rmats = [rmat]
    offsets = [sec - shift_by + 1]
    extended = with_halo(psi, (("narrow", 0),), 1)
    item = 0
    psi_src = lax.dynamic_index_in_dim(extended, offsets[item], 0, keepdims=False)
    inners = [jnp.dot(lmats[item], psi_src, precision=lax.Precision.HIGHEST)]
    sec = 0
    chan = 0
    item = chan * sec_local + sec
    total = jnp.dot(inners[item], rmats[item].T, precision=lax.Precision.HIGHEST)
    sector_terms = [total]
    terms = jnp.stack(sector_terms)
    share = lax.psum_scatter(terms, "wide", scatter_dimension=1, tiled=True)
    psi_mine = lax.dynamic_slice_in_dim(psi, wide_pos * band, band, 1)
    denominator = jnp.sum(psi_mine * psi_mine)
    numerator = jnp.sum(psi_mine * share)
    numerator, denominator = lax.psum((numerator, denominator), ("wide", "narrow"))
    alpha = numerator / denominator
    return (share - alpha * psi_mine, alpha)


def solution(mesh):
    placed = (
        P("narrow", None, None),
        P("wide", "narrow", None, None),
        P("wide", "narrow", None, None),
        P(),
        P(),
        P("wide"),
    )
    return jax.shard_map(
        per_device,
        mesh=mesh,
        in_specs=placed,
        out_specs=(P("narrow", "wide", None), P()),
        check_vma=False,
    )
```

profile of v0, /device:TPU:1, one launch (start us, length us, event | category | flops | bytes accessed | tf_op | source)
XLA Modules:
  0.0 554.6 jit_solution(10095569989408396676)
XLA Ops:
  7.2 0.0 reduce-scatter.2.cloned.1.call-start
  7.9 1.4 fusion.23
  9.3 0.6 fusion.18
  9.9 0.7 fusion.16
  10.6 0.0 copy-start.1
  10.6 1.5 multiply_multiply_fusion
  12.0 16.8 %collective-permute-start = (f32[1,512,512]{2,1,0:T(8,128)S(1)}, f32[1,512,512]{2,1,0:T(8,128)S(1)}, u32[]{:S(2)}, u32[]{:S(2)}) collective-permute-start(f32[1,512,512]{2,1,0:T(8,128)S(1)} %multiply_multiply_fusion), channel_id=1, source_target_pairs={{0,1},{1,2},{2,3},{3,4},{4,5},{5,6},{6,7},{7,8},{8,9},{9,10},{10,1... | collective-permute-start | bytes 3145736 | tf_op jit(solution)/shard_map/ppermute | solution.py:15
  28.9 1.9 collective-permute-start.1
  30.8 0.7 fusion.17
  31.5 0.7 fusion.19
  32.2 0.0 copy-start
  32.2 26.9 %collective-permute-done = f32[1,512,512]{2,1,0:T(8,128)S(1)} collective-permute-done((f32[1,512,512]{2,1,0:T(8,128)S(1)}, f32[1,512,512]{2,1,0:T(8,128)S(1)}, u32[]{:S(2)}, u32[]{:S(2)}) %collective-permute-start) | collective-permute-done | bytes 1048608 | tf_op jit(solution)/shard_map/ppermute | solution.py:15
  59.1 73.4 %collective-permute-done.1 = f32[1,512,512]{2,1,0:T(8,128)} collective-permute-done((f32[1,512,512]{2,1,0:T(8,128)S(1)}, f32[1,512,512]{2,1,0:T(8,128)}, u32[]{:S(2)}, u32[]{:S(2)}) %collective-permute-start.1) | collective-permute-done | bytes 1048608 | tf_op jit(solution)/shard_map/ppermute | solution.py:17
  132.5 0.0 copy-done.1
  132.5 3.3 fusion.3
  135.8 0.0 copy-done
  135.8 3.0 convolution_bitcast_fusion
  138.8 0.0 reduce-scatter.2.cloned.1.call-update
  138.8 0.1 dynamic-slice.5
  138.9 1.4 multiply_reduce_fusion
  140.3 222.8 %reduce-scatter.2.cloned.1.call-done = f32[1,16,512]{2,1,0:T(8,128)} async-done(((f32[1,512,512]{2,1,0:T(8,128)}), f32[1,16,512]{2,1,0:T(8,128)}) %reduce-scatter.2.cloned.1.call-update) | async-done | bytes 32784 | tf_op jit(solution)/shard_map/reduce_scatter | solution.py:72
  363.1 1.5 fusion.15
  364.5 179.2 %all-reduce = (f32[]{:T(128)}, f32[]{:T(128)}) all-reduce(f32[]{:T(128)} %fusion.15, f32[]{:T(128)} %multiply_reduce_fusion), channel_id=1, replica_groups=mesh['wide'=32,'narrow'=32] {'wide','narrow'}, use_global_device_ids=true, to_apply=%region_6.7 | all-reduce | flops 2 | bytes 16 | tf_op jit(solution)/shard_map/psum | solution.py:76
  545.1 1.5 bitcast_subtract_fusion
Async XLA Ops:
  7.2 355.9 %reduce-scatter.2.cloned.1.call-start = ((), (), s32[]{:S(2)}) async-start(), calls=%async_computation.1 | async-start | bytes 1081344 | tf_op jit(solution)/shard_map/reduce_scatter | solution.py:72
  10.6 121.9 %copy-start.1 = (f32[1,1,512,512]{3,2,1,0:T(8,128)S(1)}, f32[1,1,512,512]{3,2,1,0:T(8,128)}, u32[]{:S(2)}) copy-start(f32[1,1,512,512]{3,2,1,0:T(8,128)} %param.7) | copy-start | bytes 3145732
  12.0 47.0 %collective-permute-start = (f32[1,512,512]{2,1,0:T(8,128)S(1)}, f32[1,512,512]{2,1,0:T(8,128)S(1)}, u32[]{:S(2)}, u32[]{:S(2)}) collective-permute-start(f32[1,512,512]{2,1,0:T(8,128)S(1)} %multiply_multiply_fusion), channel_id=1, source_target_pairs={{0,1},{1,2},{2,3},{3,4},{4,5},{5,6},{6,7},{7,8},{8,9},{9,10},{10,1... | collective-permute-start | bytes 3145736 | tf_op jit(solution)/shard_map/ppermute | solution.py:15
  28.9 103.6 %collective-permute-start.1 = (f32[1,512,512]{2,1,0:T(8,128)S(1)}, f32[1,512,512]{2,1,0:T(8,128)}, u32[]{:S(2)}, u32[]{:S(2)}) collective-permute-start(f32[1,512,512]{2,1,0:T(8,128)S(1)} %multiply_multiply_fusion), channel_id=1, source_target_pairs={{1,0},{2,1},{3,2},{4,3},{5,4},{6,5},{7,6},{8,7},{9,8},{10,9},{11,1... | collective-permute-start | bytes 3145736 | tf_op jit(solution)/shard_map/ppermute | solution.py:17
  32.2 103.6 %copy-start = (f32[1,1,512,512]{3,2,1,0:T(8,128)S(1)}, f32[1,1,512,512]{3,2,1,0:T(8,128)}, u32[]{:S(2)}) copy-start(f32[1,1,512,512]{3,2,1,0:T(8,128)} %param.8) | copy-start | bytes 3145732
Sparse Core Ops, SparseCore 0:
  138.9 224.1 reduce-scatter.1
where the time goes:
time: 555 us
  waiting for transfers between devices  323 us (58%)
  blocking collectives  179 us (32%)
  starting transfers between devices  18.8 us (3%)
  between operations  17.3 us (3%)
  other arithmetic  9.86 us (2%)
  matrix products  6.28 us (1%)
    reduce_scatter x1, waiting for transfers between devices, per_device(): share = lax.psum_scatter(terms, 'wide', scatter_dimension=1, tiled=True)  223 us
    psum x1, blocking collectives, per_device(): lax.psum((numerator, denominator), ('wide', 'narrow'))  179 us
    ppermute x1, waiting for transfers between devices, with_halo(): lax.ppermute(head, axis, [((i + 1) % count, i) for i in range(ends)])  73.4 us
    ppermute x1, waiting for transfers between devices, with_halo(): lax.ppermute(tail, axis, [(i, (i + 1) % count) for i in range(ends)])  26.9 us
    ppermute x1, starting transfers between devices, with_halo(): lax.ppermute(tail, axis, [(i, (i + 1) % count) for i in range(ends)])  16.8 us
  transfers between devices with their start and end apart: 3, of which 3 were waited for; matrix products, arithmetic and copies ran while one was open for 1% of the time, Pallas kernels for 0%

commit v1 on v0

v1 whole, which is shorter than its diff:
```python
import functools

import jax
import jax.numpy as jnp
from jax import lax
from jax.experimental import pallas as pl
from jax.experimental.pallas import tpu as pltpu
from jax.sharding import PartitionSpec as P

MESH = pl.DeviceIdType.MESH
F32 = jnp.float32
BF16 = jnp.bfloat16

NX = 4
NJ = 8
NQ = 4
NR = 4
NC = 2


def split(v):
    high = v.astype(BF16)
    return high, (v - high.astype(F32)).astype(BF16)


def product(ah, al, bh, bl, dims):
    dot = functools.partial(
        lax.dot_general, dimension_numbers=(dims, ((), ())), preferred_element_type=F32
    )
    return dot(ah, bh) + (dot(ah, bl) + dot(al, bh))


def kernel(
    state, left, right, lsizes, rsizes, charge,
    out, alpha_out,
    own, lenv, renv, near, far, ph, plo, rh, rl, term,
    from_left, from_right, zsum, zrecv, g1, g2, g3,
    local_sem, send_sem, recv_sem,
):
    size = own.shape[0]
    band = size // (NX * NJ)
    block = band * NJ
    half = block // 2
    quarter = half // 2
    w = lax.axis_index("wide")
    n = lax.axis_index("narrow")
    x, j = w // NJ, w % NJ
    q, r, c = n // (NR * NC), (n // NC) % NR, n % NC
    total_n = NQ * NR * NC

    def at_x(step):
        return (lax.rem(x + step, NX) * NJ + j, n)

    def at_j(other):
        return (x * NJ + other, n)

    def at_qr(step):
        qr = lax.rem(q * NR + r + step, NQ * NR)
        return (w, qr * NC + c)

    def at_xc(step):
        xc = lax.rem(x * NC + c + step, NX * NC)
        return ((xc // NC) * NJ + j, (q * NR + r) * NC + xc % NC)

    sibling = (w, n + 1 - 2 * c)
    across = (w, lax.rem(n + 2 * c - 1 + total_n, total_n))

    own_copy = pltpu.make_async_copy(state, own, local_sem.at[0])
    left_copy = pltpu.make_async_copy(left, lenv, local_sem.at[1])
    right_copy = pltpu.make_async_copy(right, renv, local_sem.at[2])
    right_copy.start()
    own_copy.start()
    left_copy.start()

    barrier = pltpu.get_barrier_semaphore()
    partners = (
        [across]
        + [at_j(lax.rem(j + s, NJ)) for s in range(1, NJ)]
        + [at_xc(s) for s in range(1, NX * NC)]
        + [at_qr(s) for s in range(1, NQ * NR)]
    )
    for partner in partners:
        pl.semaphore_signal(barrier, inc=1, device_id=partner, device_id_type=MESH)
    pl.semaphore_wait(barrier, len(partners))

    started = []

    def push(src, dst, device):
        i = len(started)
        copy = pltpu.make_async_remote_copy(
            src_ref=src, dst_ref=dst, send_sem=send_sem.at[i], recv_sem=recv_sem.at[i],
            device_id=device, device_id_type=MESH,
        )
        copy.start()
        started.append(copy)
        return copy

    pos = (j % 2) * 4 + (j // 2 % 2) * 2 + j // 4
    base = x * block

    def rows(start, count):
        return pl.ds(pl.multiple_of(start, 8), count)

    shard = rows(base + pos * band, band)
    cross = push(state.at[shard], far.at[shard], across)
    nearby = push(state, near, sibling)

    right_copy.wait()
    slab = 32

    @pl.loop(0, size // slab)
    def _(i):
        at = rows(i * slab, slab)
        rh[at], rl[at] = split(renv[at])

    own_copy.wait()
    rows_own, cols_own = lsizes[n], rsizes[n]

    def masked(values, first, rlimit, climit):
        rid = lax.broadcasted_iota(jnp.int32, values.shape, 0) + first
        cid = lax.broadcasted_iota(jnp.int32, values.shape, 1)
        return jnp.where((rid < rlimit) & (cid < climit), values, 0.0)

    def lanes(values):
        s = jnp.sum(values, axis=0, keepdims=True)
        return s[:, 0:128] + s[:, 128:256] + s[:, 256:384] + s[:, 384:512]

    def square(i, total):
        at = rows(i * slab, slab)
        psi = masked(own[at], i * slab, rows_own, cols_own)
        own[at] = psi
        return total + lanes(psi * psi)

    den = lax.fori_loop(0, size // slab, square, jnp.zeros((1, 128), F32))
    den = jnp.where(w == 0, den, 0.0)

    def part(xb, start, count):
        return rows(xb * block + start, count)

    x1, x2, x3 = lax.rem(x + 1, NX), lax.rem(x + 2, NX), lax.rem(x + 3, NX)

    cross.wait_recv()
    first = push(far.at[shard], far.at[shard], at_j(j + 4 - 8 * (j // 4)))
    first.wait_recv()
    at2 = rows(base + (pos // 2) * 2 * band, 2 * band)
    second = push(far.at[at2], far.at[at2], at_j(j + 2 - 4 * (j // 2 % 2)))
    second.wait_recv()
    lo = (pos // 4) * half
    hi = half - lo
    at3 = rows(base + lo, half)
    third = push(far.at[at3], far.at[at3], at_j(j + 1 - 2 * (j % 2)))
    right_lo = push(far.at[at3], far.at[at3], at_x(1))
    left_lo = push(far.at[at3], far.at[at3], at_x(3))
    third.wait_recv()
    at4 = rows(base + hi, half)
    right_hi = push(far.at[at4], far.at[at4], at_x(1))
    left_hi = push(far.at[at4], far.at[at4], at_x(3))
    right_lo.wait_recv()
    piece = part(x3, lo, quarter)
    relay_right_lo = push(far.at[piece], far.at[piece], at_x(1))
    left_lo.wait_recv()
    piece = part(x1, lo + quarter, quarter)
    relay_left_lo = push(far.at[piece], far.at[piece], at_x(3))
    right_hi.wait_recv()
    piece = part(x3, hi, quarter)
    relay_right_hi = push(far.at[piece], far.at[piece], at_x(1))
    left_hi.wait_recv()
    piece = part(x1, hi + quarter, quarter)
    relay_left_hi = push(far.at[piece], far.at[piece], at_x(3))
    nearby.wait_recv()
    left_copy.wait()
    relay_right_lo.wait_recv()
    relay_left_lo.wait_recv()
    relay_right_hi.wait_recv()
    relay_left_hi.wait_recv()

    shift = charge[0] - 1
    source = n - shift
    clipped = jnp.clip(source, 0, total_n - 1)
    inside = (source == clipped).astype(jnp.int32)
    rows_src, cols_src = lsizes[clipped] * inside, rsizes[clipped] * inside
    toward = shift * (1 - 2 * c)

    @pl.loop(0, size // slab)
    def _(i):
        at = rows(i * slab, slab)
        took = jnp.where(toward == 1, far[at], jnp.where(toward == 0, own[at], near[at]))
        ph[at], plo[at] = split(masked(took, i * slab, rows_src, cols_src))

    num = jnp.zeros((1, 128), F32)

    def compute(xb, num):
        at = part(xb, 0, block)
        lh, ll = split(lenv[at])
        inner = product(lh, ll, ph[...], plo[...], ((1,), (0,)))
        ih, il = split(inner)
        t = product(ih, il, rh[...], rl[...], ((1,), (1,)))
        t = masked(t, xb * block, rows_own, cols_own)
        term[at] = t
        return num + lanes(t * own[at])

    num = compute(x2, num)
    r1 = push(term.at[part(x2, 0, half)], from_left.at[0], at_x(1))
    l1 = push(term.at[part(x2, half, half)], from_right.at[0], at_x(3))
    num = compute(x1, num)
    r2 = push(term.at[part(x1, half, half)], from_left.at[1], at_x(1))
    num = compute(x3, num)
    l2 = push(term.at[part(x3, 0, half)], from_right.at[1], at_x(3))
    num = compute(x, num)

    g1[j] = jnp.concatenate([num, den], axis=1)
    c1 = [push(g1.at[j], g1.at[j], at_j(lax.rem(j + s, NJ))) for s in range(1, NJ)]

    r1.wait_recv()
    at = part(x1, 0, half)
    term[at] += from_left[0]
    r3 = push(term.at[at], from_left.at[2], at_x(1))
    l1.wait_recv()
    at = part(x3, half, half)
    term[at] += from_right[0]
    l3 = push(term.at[at], from_right.at[2], at_x(3))

    for copy in c1:
        copy.wait_recv()
    xc = x * NC + c
    s1 = g1[0]
    for i in range(1, NJ):
        s1 = s1 + g1[i]
    g2[xc] = s1
    c2 = [push(g2.at[xc], g2.at[xc], at_xc(s)) for s in range(1, NX * NC)]

    r2.wait_recv()
    l2.wait_recv()
    r3.wait_recv()
    zsum[0:half] = term[part(x, 0, half)] + from_left[2] + from_right[1]
    l3.wait_recv()
    zsum[half:block] = term[part(x, half, half)] + from_left[1] + from_right[2]
    zs = []
    for s in (4, 3, 5, 2, 6, 1, 7):
        other = lax.rem(j + s, NJ)
        zs.append(push(zsum.at[rows(other * band, band)], zrecv.at[j], at_j(other)))

    for copy in c2:
        copy.wait_recv()
    qr = q * NR + r
    s2 = g2[0]
    for i in range(1, NX * NC):
        s2 = s2 + g2[i]
    g3[qr] = s2
    c3 = [push(g3.at[qr], g3.at[qr], at_qr(s)) for s in range(1, NQ * NR)]

    zrecv[j] = zsum[rows(j * band, band)]
    for copy in c3:
        copy.wait_recv()
    s3 = g3[0]
    for i in range(1, NQ * NR):
        s3 = s3 + g3[i]
    alpha = jnp.sum(s3[:, 0:128], axis=1, keepdims=True) / jnp.sum(
        s3[:, 128:256], axis=1, keepdims=True
    )
    alpha_out[...] = alpha
    for copy in zs:
        copy.wait_recv()
    share = zrecv[0]
    for i in range(1, NJ):
        share = share + zrecv[i]
    out[...] = share - alpha * own[rows(w * band, band)]
    for copy in started:
        copy.wait_send()


COPIES = 2 + 3 + 8 + 6 + (NJ - 1) * 2 + (NX * NC - 1) + (NQ * NR - 1)


def per_device(state, left_env, right_env, left_sizes, right_sizes, channel_charge):
    size = state.shape[1]
    band = size // (NX * NJ)
    block = band * NJ
    hbm = pl.BlockSpec(memory_space=pl.ANY)
    smem = pl.BlockSpec(memory_space=pltpu.SMEM)
    vmem = pl.BlockSpec(memory_space=pltpu.VMEM)
    full = (size, size)
    share, alpha = pl.pallas_call(
        kernel,
        out_shape=(
            jax.ShapeDtypeStruct((band, size), F32),
            jax.ShapeDtypeStruct((1, 1), F32),
        ),
        in_specs=[hbm, hbm, hbm, smem, smem, smem],
        out_specs=(vmem, vmem),
        scratch_shapes=[
            pltpu.VMEM(full, F32),
            pltpu.VMEM(full, F32),
            pltpu.VMEM(full, F32),
            pltpu.VMEM(full, F32),
            pltpu.VMEM(full, F32),
            pltpu.VMEM(full, BF16),
            pltpu.VMEM(full, BF16),
            pltpu.VMEM(full, BF16),
            pltpu.VMEM(full, BF16),
            pltpu.VMEM(full, F32),
            pltpu.VMEM((3, block // 2, size), F32),
            pltpu.VMEM((3, block // 2, size), F32),
            pltpu.VMEM((block, size), F32),
            pltpu.VMEM((NJ, band, size), F32),
            pltpu.VMEM((NJ, 1, 256), F32),
            pltpu.VMEM((NX * NC, 1, 256), F32),
            pltpu.VMEM((NQ * NR, 1, 256), F32),
            pltpu.SemaphoreType.DMA((3,)),
            pltpu.SemaphoreType.DMA((COPIES,)),
            pltpu.SemaphoreType.DMA((COPIES,)),
        ],
        compiler_params=pltpu.CompilerParams(
            collective_id=0, has_side_effects=True, vmem_limit_bytes=60 << 20
        ),
    )(state[0], left_env[0, 0], right_env[0, 0], left_sizes, right_sizes, channel_charge)
    return share[None], alpha[0, 0]


def solution(mesh):
    placed = (
        P("narrow", None, None),
        P("wide", "narrow", None, None),
        P("wide", "narrow", None, None),
        P(),
        P(),
        P("wide"),
    )
    return jax.shard_map(
        per_device,
        mesh=mesh,
        in_specs=placed,
        out_specs=(P("narrow", "wide", None), P()),
        check_vma=False,
    )
```

time: 555 us -> 93 us (0.17)
  waiting for transfers between devices: 323 us -> 0 us
  blocking collectives: 179 us -> 0 us
  Pallas kernels: 0 us -> 88.3 us
  starting transfers between devices: 18.8 us -> 0 us
  between operations: 17.3 us -> 3.05 us
  other arithmetic: 9.86 us -> 0 us
  matrix products: 6.28 us -> 0 us
    reduce_scatter x1 -> x0, waiting for transfers between devices: 223 us -> none  [per_device(): share = lax.psum_scatter(terms, 'wide', scatter_dimension=1, tiled=True)]
    psum x1 -> x0, blocking collectives: 179 us -> none  [per_device(): lax.psum((numerator, denominator), ('wide', 'narrow'))]
    ppermute x2 -> x0, waiting for transfers between devices: 100 us -> none  [the longest x1 73.4 us: with_halo(): lax.ppermute(head, axis, [((i + 1) % count, i) for i in range(ends)])]
    pallas_call x0 -> x1, Pallas kernels: none -> 88.3 us  [per_device(): pl.pallas_call(kernel, out_shape=(jax.ShapeDtypeStruct((band, size), F32)...]
    ppermute x2 -> x0, starting transfers between devices: 18.8 us -> none  [the longest x1 16.8 us: with_halo(): lax.ppermute(tail, axis, [(i, (i + 1) % count) for i in range(ends)])]
    dot_general x2 -> x0, matrix products: 6.28 us -> none  [the longest x1 3.29 us: per_device(): inners = [jnp.dot(lmats[item], psi_src, precision=lax.Precision.HIGHEST)]]
  transfers between devices with their start and end apart: 3 -> 0, of which waited for: 3 -> 0; matrix products, arithmetic and copies ran while one was open for 1% -> 0% of each run, Pallas kernels for 0% -> 0%
where the time goes in v1:
time: 93 us; the launch traced here: 92.7 us
  Pallas kernels  88.3 us (95%)
  between operations  3.05 us (3%)
  local copies, waits for them, and re-layouts  1.38 us (1%)
    pallas_call x1, Pallas kernels, per_device(): pl.pallas_call(kernel, out_shape=(jax.ShapeDtypeStruct((band, size), F32)...  88.3 us

profile of v1, /device:TPU:1, one launch (start us, length us, event | category | flops | bytes accessed | tf_op | source)
XLA Modules:
  0.0 92.7 jit_solution(16902814074448997589)
XLA Ops:
  1.3 88.3 %shard_map.77 = (f32[16,512]{1,0:T(8,128)}, f32[1,1]{1,0:T(1,128)}) custom-call(f32[512,512]{1,0:T(8,128)} %bitcast.5, f32[512,512]{1,0:T(8,128)} %bitcast.6, f32[512,512]{1,0:T(8,128)} %bitcast.7, s32[32]{0:T(128)} %lsizes.1, s32[32]{0:T(128)} %rsizes.1, s32[1]{0:T(128)S(6)} %copy.10.charge), custom_call_target="tpu_custom_call" | custom-call | tf_op jit(solution)/shard_map/pallas_call | solution.py:283
  89.6 1.4 %copy.11 = f32[1,16,512]{2,1,0:T(8,128)} copy(f32[1,16,512]{2,1,0:T(8,128)} %bitcast.8) | data formatting | bytes 65536

commit v2 on v1

v2 whole, which is shorter than its diff:
```python
import functools

import jax
import jax.numpy as jnp
from jax import lax
from jax.experimental import pallas as pl
from jax.experimental.pallas import tpu as pltpu
from jax.sharding import PartitionSpec as P

MESH = pl.DeviceIdType.MESH
F32 = jnp.float32
BF16 = jnp.bfloat16

NX = 4
NJ = 8
NQ = 4
NR = 4
NC = 2
LANES = 128
COPIES = 72


def split(v):
    high = v.astype(BF16)
    return high, (v - high.astype(F32)).astype(BF16)


def product(ah, al, bh, bl):
    dot = functools.partial(jnp.dot, preferred_element_type=F32)
    return dot(ah, bh) + (dot(ah, bl) + dot(al, bh))


def kernel(
    state, left, right, lsizes, rsizes, charge,
    result,
    own, lenv, renv, near, far, lh, ll, rh, rl, ph, plo, ih, il, term,
    from_x, zsum, zrecv, g1, g2, g3,
    local_sem, send_sem, recv_sem,
):
    size = own.shape[0]
    band = size // (NX * NJ)
    block = band * NJ
    pair = 2 * band
    tall = size // NJ
    w = lax.axis_index("wide")
    n = lax.axis_index("narrow")
    x, j = w // NJ, w % NJ
    h, i = j // 4, j % 4
    q, r, c = n // (NR * NC), (n // NC) % NR, n % NC
    total_n = NQ * NR * NC

    def at_x(step):
        return (lax.rem(x + step, NX) * NJ + j, n)

    def at_j(other):
        return (x * NJ + other, n)

    def at_qr(step):
        qr = lax.rem(q * NR + r + step, NQ * NR)
        return (w, qr * NC + c)

    def at_xc(step):
        xc = lax.rem(x * NC + c + step, NX * NC)
        return ((xc // NC) * NJ + j, (q * NR + r) * NC + xc % NC)

    over = lax.rem(n + 2 * c - 1 + total_n, total_n)
    sibling = (w, n + 1 - 2 * c)
    across = (w, over)
    across_four = (x * NJ + (1 - h) * 4 + i, over)
    quad = [i + 1 - 2 * (i % 2), i + 2 - 4 * (i // 2), 3 - i]

    own_copy = pltpu.make_async_copy(state, own, local_sem.at[0])
    left_copy = pltpu.make_async_copy(left, lenv, local_sem.at[1])
    right_copy = pltpu.make_async_copy(right, renv, local_sem.at[2])

    barrier = pltpu.get_barrier_semaphore()
    partners = (
        [across, across_four]
        + [at_qr(s) for s in range(1, NQ * NR)]
        + [at_j(lax.rem(j + s, NJ)) for s in range(1, NJ)]
        + [at_xc(s) for s in range(1, NX * NC)]
    )
    for partner in partners:
        pl.semaphore_signal(barrier, inc=1, device_id=partner, device_id_type=MESH)
    right_copy.start()
    own_copy.start()
    left_copy.start()
    pl.semaphore_wait(barrier, len(partners))

    started = []

    def push(src, dst, device):
        i = len(started)
        copy = pltpu.make_async_remote_copy(
            src_ref=src, dst_ref=dst, send_sem=send_sem.at[i], recv_sem=recv_sem.at[i],
            device_id=device, device_id_type=MESH,
        )
        copy.start()
        started.append(copy)
        return copy

    def rows(start, count):
        return pl.ds(pl.multiple_of(start, 8), count)

    def cols(xb):
        return pl.ds(pl.multiple_of(xb * LANES, LANES), LANES)

    piece = state.at[rows(j * tall, tall), cols(x)]
    cross = push(piece, far.at[h, i, :, cols(x)], across)
    cross_four = push(piece, far.at[h, i, :, cols(x)], across_four)
    nearby = push(state, near, sibling)

    slab = 32
    right_copy.wait()
    for t in range(size // LANES):
        at = pl.ds(t * LANES, LANES)
        rh[at, :], rl[at, :] = split(renv[:, at].T)

    left_copy.wait()

    @pl.loop(0, size // slab)
    def _(t):
        at = rows(t * slab, slab)
        lh[at], ll[at] = split(lenv[at])

    own_copy.wait()
    rows_own, cols_own = lsizes[n], rsizes[n]

    def masked(values, first, across_first, rlimit, climit):
        rid = lax.broadcasted_iota(jnp.int32, values.shape, 0) + first
        cid = lax.broadcasted_iota(jnp.int32, values.shape, 1) + across_first
        return jnp.where((rid < rlimit) & (cid < climit), values, 0.0)

    def lanes(values):
        s = jnp.sum(values, axis=0, keepdims=True)
        return s[:, 0:128] + s[:, 128:256] + s[:, 256:384] + s[:, 384:512]

    def square(t, total):
        at = rows(t * slab, slab)
        psi = masked(own[at], t * slab, 0, rows_own, cols_own)
        own[at] = psi
        return total + lanes(psi * psi)

    den = lax.fori_loop(0, size // slab, square, jnp.zeros((1, LANES), F32))
    den = jnp.where(w == 0, den, 0.0)

    shift = charge[0] - 1
    source = n - shift
    clipped = jnp.clip(source, 0, total_n - 1)
    inside = (source == clipped).astype(jnp.int32)
    rows_src, cols_src = lsizes[clipped] * inside, rsizes[clipped] * inside
    toward = shift * (1 - 2 * c)

    def along(src):
        return [push(src, src, at_x(s)) for s in range(1, NX)]

    cross.wait_recv()
    mine = far.at[h, i, :, cols(x)]
    quad_one = [push(mine, mine, at_j(h * 4 + to)) for to in quad]
    sent = [along(mine)]
    cross_four.wait_recv()
    mine = far.at[1 - h, i, :, cols(x)]
    quad_two = [push(mine, mine, at_j(h * 4 + to)) for to in quad]
    sent.append(along(mine))
    for one, two, to in zip(quad_one, quad_two, quad):
        one.wait_recv()
        two.wait_recv()
        sent.append(along(far.at[:, to, :, cols(x)]))

    def inner(xb):
        at = cols(xb)
        for t in range(NJ):
            down = pl.ds(t * tall, tall)
            took = jnp.where(
                toward == 1, far[t // 4, t % 4, :, at],
                jnp.where(toward == 0, own[down, at], near[down, at]),
            )
            took = masked(took, t * tall, xb * LANES, rows_src, cols_src)
            ph[down], plo[down] = split(took)
        ih[:, at], il[:, at] = split(product(lh[...], ll[...], ph[...], plo[...]))

    x1, x2, x3 = lax.rem(x + 1, NX), lax.rem(x + 2, NX), lax.rem(x + 3, NX)
    nearby.wait_recv()
    inner(x)
    for s, xb in ((1, x3), (3, x1), (2, x2)):
        for copies in sent:
            copies[s - 1].wait_recv()
        inner(xb)

    num = jnp.zeros((1, LANES), F32)
    for xb in (x2, x1, x3, x):
        at = rows(xb * block, block)
        t = product(ih[at], il[at], rh[...], rl[...])
        t = masked(t, xb * block, 0, rows_own, cols_own)
        term[at] = t
        num = num + lanes(t * own[at])

    g1[j] = jnp.concatenate([num, den], axis=1)
    c1 = [push(g1.at[j], g1.at[j], at_j(lax.rem(j + s, NJ))) for s in range(1, NJ)]

    u = j // 2
    places = [3 - u, u + 2 - 4 * (u // 2), u + 1 - 2 * (u % 2), u]

    def scatter(place):
        return [
            push(
                term.at[rows(xb * block + place * pair, pair)],
                from_x.at[s - 1, rows(place * pair, pair)], at_x(s),
            )
            for s, xb in ((2, x2), (1, x1), (3, x3))
        ]

    pieces = [scatter(places[0])]
    for copy in c1:
        copy.wait_recv()
    xc = x * NC + c
    s1 = g1[0]
    for t in range(1, NJ):
        s1 = s1 + g1[t]
    g2[xc] = s1
    c2 = [push(g2.at[xc], g2.at[xc], at_xc(s)) for s in range(1, NX * NC)]
    pieces.append(scatter(places[1]))
    for copy in c2:
        copy.wait_recv()
    qr = q * NR + r
    s2 = g2[0]
    for t in range(1, NX * NC):
        s2 = s2 + g2[t]
    g3[qr] = s2
    c3 = [push(g3.at[qr], g3.at[qr], at_qr(s)) for s in range(1, NQ * NR)]
    pieces.append(scatter(places[2]))
    pieces.append(scatter(places[3]))

    zs = []
    for place, copies in zip(places, pieces):
        for copy in copies:
            copy.wait_recv()
        at = rows(place * pair, pair)
        zsum[at] = (term[rows(x * block + place * pair, pair)] + from_x[0, at]) + (
            from_x[1, at] + from_x[2, at]
        )
        odd = j % 2
        two = (2 * place + odd, 2 * place + 1 - odd) if place is not u else (j + 1 - 2 * odd,)
        for other in two:
            zs.append(push(zsum.at[rows(other * band, band)], zrecv.at[j], at_j(other)))
    zrecv[j] = zsum[rows(j * band, band)]
    for copy in zs:
        copy.wait_recv()
    share = zrecv[0]
    for t in range(1, NJ):
        share = share + zrecv[t]
    mine = own[rows(w * band, band)]
    for copy in c3:
        copy.wait_recv()
    s3 = g3[0]
    for t in range(1, NQ * NR):
        s3 = s3 + g3[t]
    alpha = jnp.sum(s3[:, 0:LANES], axis=1, keepdims=True) / jnp.sum(
        s3[:, LANES:], axis=1, keepdims=True
    )
    result[0:band] = share - alpha * mine
    result[band:band + 8] = jnp.broadcast_to(alpha, (8, size))
    for copy in started:
        copy.wait_send()


def finish(result, out, alpha):
    band = out.shape[0]
    out[...] = result[0:band]
    alpha[...] = result[band:band + 1, 0:1]


def per_device(state, left_env, right_env, left_sizes, right_sizes, channel_charge):
    size = state.shape[1]
    band = size // (NX * NJ)
    block = band * NJ
    hbm = pl.BlockSpec(memory_space=pl.ANY)
    smem = pl.BlockSpec(memory_space=pltpu.SMEM)
    vmem = pl.BlockSpec(memory_space=pltpu.VMEM)
    full = (size, size)
    result = pl.pallas_call(
        kernel,
        out_shape=jax.ShapeDtypeStruct((band + 8, size), F32),
        in_specs=[hbm, hbm, hbm, smem, smem, smem],
        out_specs=vmem,
        scratch_shapes=[
            pltpu.VMEM(full, F32),
            pltpu.VMEM(full, F32),
            pltpu.VMEM(full, F32),
            pltpu.VMEM(full, F32),
            pltpu.VMEM((2, 4, size // NJ, size), F32),
            pltpu.VMEM(full, BF16),
            pltpu.VMEM(full, BF16),
            pltpu.VMEM(full, BF16),
            pltpu.VMEM(full, BF16),
            pltpu.VMEM((size, LANES), BF16),
            pltpu.VMEM((size, LANES), BF16),
            pltpu.VMEM(full, BF16),
            pltpu.VMEM(full, BF16),
            pltpu.VMEM(full, F32),
            pltpu.VMEM((NX - 1, block, size), F32),
            pltpu.VMEM((block, size), F32),
            pltpu.VMEM((NJ, band, size), F32),
            pltpu.VMEM((NJ, 1, 2 * LANES), F32),
            pltpu.VMEM((NX * NC, 1, 2 * LANES), F32),
            pltpu.VMEM((NQ * NR, 1, 2 * LANES), F32),
            pltpu.SemaphoreType.DMA((3,)),
            pltpu.SemaphoreType.DMA((COPIES,)),
            pltpu.SemaphoreType.DMA((COPIES,)),
        ],
        compiler_params=pltpu.CompilerParams(
            collective_id=0, has_side_effects=True, vmem_limit_bytes=60 << 20
        ),
    )(state[0], left_env[0, 0], right_env[0, 0], left_sizes, right_sizes, channel_charge)
    share, alpha = pl.pallas_call(
        finish,
        out_shape=(
            jax.ShapeDtypeStruct((band, size), F32),
            jax.ShapeDtypeStruct((1, 1), F32),
        ),
        in_specs=[vmem],
        out_specs=(vmem, vmem),
    )(result)
    return share[None], alpha[0, 0]


def solution(mesh):
    placed = (
        P("narrow", None, None),
        P("wide", "narrow", None, None),
        P("wide", "narrow", None, None),
        P(),
        P(),
        P("wide"),
    )
    return jax.shard_map(
        per_device,
        mesh=mesh,
        in_specs=placed,
        out_specs=(P("narrow", "wide", None), P()),
        check_vma=False,
    )
```

time: 93 us -> 86 us (0.925)
  Pallas kernels: 88.3 us -> 84 us
  between operations: 3.05 us -> 1.29 us
  local copies, waits for them, and re-layouts: 1.38 us -> 0 us
    pallas_call x1 -> x2, Pallas kernels: 88.3 us -> 84 us  [the longest x1 82.6 us: per_device(): pl.pallas_call(kernel, out_shape=jax.ShapeDtypeStruct((band + 8, size), F...]
    unnamed x1 -> x0, local copies, waits for them, and re-layouts: 1.38 us -> none
where the time goes in v2:
time: 86 us; the launch traced here: 85.3 us
  Pallas kernels  84 us (98%)
  between operations  1.29 us (2%)
    pallas_call x1, Pallas kernels, per_device(): pl.pallas_call(kernel, out_shape=jax.ShapeDtypeStruct((band + 8, size), F...  82.6 us

profile of v2, /device:TPU:1, one launch (start us, length us, event | category | flops | bytes accessed | tf_op | source)
XLA Modules:
  0.0 85.3 jit_solution(18081579276223544132)
XLA Ops:
  1.3 82.6 %shard_map.77.result = f32[24,512]{1,0:T(8,128)} custom-call(f32[512,512]{1,0:T(8,128)} %bitcast.5, f32[512,512]{1,0:T(8,128)} %bitcast.6, f32[512,512]{1,0:T(8,128)} %bitcast.7, s32[32]{0:T(128)} %lsizes.1, s32[32]{0:T(128)} %rsizes.1, s32[1]{0:T(128)S(6)} %copy.8.charge), custom_call_target="tpu_custom_call" | custom-call | tf_op jit(solution)/shard_map/pallas_call | solution.py:281
  83.9 1.4 %shard_map.78 = (f32[16,512]{1,0:T(8,128)}, f32[1,1]{1,0:T(1,128)}) custom-call(f32[24,512]{1,0:T(8,128)} %shard_map.77.result), custom_call_target="tpu_custom_call" | custom-call | tf_op jit(solution)/shard_map/pallas_call | solution.py:315

commit v3 on v2

--- a/solution.py
+++ b/solution.py
@@ -17,7 +17,7 @@
 NR = 4
 NC = 2
 LANES = 128
-COPIES = 72
+COPIES = 114
 
 
 def split(v):
@@ -31,11 +31,12 @@
 
 
 def kernel(
-    state, left, right, lsizes, rsizes, charge,
+    state, folded, left, right, lsizes_in, rsizes_in, charge,
     result,
+    lsizes, rsizes,
     own, lenv, renv, near, far, lh, ll, rh, rl, ph, plo, ih, il, term,
-    from_x, zsum, zrecv, g1, g2, g3,
-    local_sem, send_sem, recv_sem,
+    from_x, zsum, zrecv, g1, g2,
+    local_sem, send_sem, recv_sem, met,
 ):
     size = own.shape[0]
     band = size // (NX * NJ)
@@ -55,36 +56,46 @@
     def at_j(other):
         return (x * NJ + other, n)
 
-    def at_qr(step):
-        qr = lax.rem(q * NR + r + step, NQ * NR)
-        return (w, qr * NC + c)
-
-    def at_xc(step):
-        xc = lax.rem(x * NC + c + step, NX * NC)
-        return ((xc // NC) * NJ + j, (q * NR + r) * NC + xc % NC)
-
-    over = lax.rem(n + 2 * c - 1 + total_n, total_n)
+    def at_xyc(step):
+        to = lax.rem((x * NQ + q) * NC + c + step, NX * NQ * NC)
+        return ((to // (NQ * NC)) * NJ + j, (to // NC % NQ * NR + r) * NC + to % NC)
+
+    def at_z(step):
+        to = lax.rem(r * NJ + j + step, NR * NJ)
+        return (x * NJ + to % NJ, (q * NR + to // NJ) * NC + c)
+
+    def at_run(step, core):
+        return (w, (q * NR + lax.rem(r + step, NR)) * NC + core)
+
     sibling = (w, n + 1 - 2 * c)
-    across = (w, over)
-    across_four = (x * NJ + (1 - h) * 4 + i, over)
+    across = (w, lax.rem(n + 2 * c - 1 + total_n, total_n))
     quad = [i + 1 - 2 * (i % 2), i + 2 - 4 * (i // 2), 3 - i]
 
     own_copy = pltpu.make_async_copy(state, own, local_sem.at[0])
     left_copy = pltpu.make_async_copy(left, lenv, local_sem.at[1])
     right_copy = pltpu.make_async_copy(right, renv, local_sem.at[2])
 
+    small = [
+        pltpu.make_async_copy(src, dst, local_sem.at[3 + t])
+        for t, (src, dst) in enumerate(
+            ((lsizes_in, lsizes), (rsizes_in, rsizes))
+        )
+    ]
+
     barrier = pltpu.get_barrier_semaphore()
     partners = (
-        [across, across_four]
-        + [at_qr(s) for s in range(1, NQ * NR)]
+        [across]
+        + [at_run(s, core) for s in (1, NR - 1) for core in range(NC)]
         + [at_j(lax.rem(j + s, NJ)) for s in range(1, NJ)]
-        + [at_xc(s) for s in range(1, NX * NC)]
+        + [at_xyc(s) for s in range(1, NX * NQ * NC)]
     )
     for partner in partners:
         pl.semaphore_signal(barrier, inc=1, device_id=partner, device_id_type=MESH)
     right_copy.start()
     own_copy.start()
     left_copy.start()
+    for copy in small:
+        copy.start()
     pl.semaphore_wait(barrier, len(partners))
 
     started = []
@@ -105,9 +116,10 @@
     def cols(xb):
         return pl.ds(pl.multiple_of(xb * LANES, LANES), LANES)
 
-    piece = state.at[rows(j * tall, tall), cols(x)]
-    cross = push(piece, far.at[h, i, :, cols(x)], across)
-    cross_four = push(piece, far.at[h, i, :, cols(x)], across_four)
+    def bands(ref, k, t):
+        return ref.at[:, k, rows(t * (tall // 2), tall // 2), cols(x)]
+
+    cross = [push(bands(folded, i, t), bands(far, i, t), across) for t in range(2)]
     nearby = push(state, near, sibling)
 
     slab = 32
@@ -124,6 +136,8 @@
         lh[at], ll[at] = split(lenv[at])
 
     own_copy.wait()
+    for copy in small:
+        copy.wait()
     rows_own, cols_own = lsizes[n], rsizes[n]
 
     def masked(values, first, across_first, rlimit, climit):
@@ -154,18 +168,17 @@
     def along(src):
         return [push(src, src, at_x(s)) for s in range(1, NX)]
 
-    cross.wait_recv()
-    mine = far.at[h, i, :, cols(x)]
-    quad_one = [push(mine, mine, at_j(h * 4 + to)) for to in quad]
-    sent = [along(mine)]
-    cross_four.wait_recv()
-    mine = far.at[1 - h, i, :, cols(x)]
-    quad_two = [push(mine, mine, at_j(h * 4 + to)) for to in quad]
-    sent.append(along(mine))
-    for one, two, to in zip(quad_one, quad_two, quad):
-        one.wait_recv()
-        two.wait_recv()
-        sent.append(along(far.at[:, to, :, cols(x)]))
+    quads, sent = [], []
+    for t in range(2):
+        cross[t].wait_recv()
+        mine = bands(far, i, t)
+        quads.append([push(mine, mine, at_j(h * 4 + to)) for to in quad])
+        sent.append(along(mine))
+    for t in range(2):
+        for copy, to in zip(quads[t], quad):
+            copy.wait_recv()
+            sent.append(along(bands(far, to, t)))
+    pl.semaphore_signal(met, inc=1, device_id=at_j((1 - h) * 4 + i), device_id_type=MESH)
 
     def inner(xb):
         at = cols(xb)
@@ -195,8 +208,10 @@
         term[at] = t
         num = num + lanes(t * own[at])
 
-    g1[j] = jnp.concatenate([num, den], axis=1)
-    c1 = [push(g1.at[j], g1.at[j], at_j(lax.rem(j + s, NJ))) for s in range(1, NJ)]
+    pl.semaphore_wait(met, 1)
+    xyc = (x * NQ + q) * NC + c
+    g1[xyc] = jnp.concatenate([num, den], axis=1)
+    c1 = [push(g1.at[xyc], g1.at[xyc], at_xyc(s)) for s in range(1, NX * NQ * NC)]
 
     u = j // 2
     places = [3 - u, u + 2 - 4 * (u // 2), u + 1 - 2 * (u % 2), u]
@@ -210,26 +225,17 @@
             for s, xb in ((2, x2), (1, x1), (3, x3))
         ]
 
-    pieces = [scatter(places[0])]
+    pieces = [scatter(place) for place in places[:2]]
     for copy in c1:
         copy.wait_recv()
-    xc = x * NC + c
+    zz = r * NJ + j
     s1 = g1[0]
-    for t in range(1, NJ):
+    for t in range(1, NX * NQ * NC):
         s1 = s1 + g1[t]
-    g2[xc] = s1
-    c2 = [push(g2.at[xc], g2.at[xc], at_xc(s)) for s in range(1, NX * NC)]
-    pieces.append(scatter(places[1]))
-    for copy in c2:
-        copy.wait_recv()
-    qr = q * NR + r
-    s2 = g2[0]
-    for t in range(1, NX * NC):
-        s2 = s2 + g2[t]
-    g3[qr] = s2
-    c3 = [push(g3.at[qr], g3.at[qr], at_qr(s)) for s in range(1, NQ * NR)]
-    pieces.append(scatter(places[2]))
-    pieces.append(scatter(places[3]))
+    g2[zz] = s1
+    farthest_first = sorted(range(1, NR * NJ), key=lambda s: -min(s, NR * NJ - s))
+    c2 = [push(g2.at[zz], g2.at[zz], at_z(s)) for s in farthest_first]
+    pieces += [scatter(place) for place in places[2:]]
 
     zs = []
     for place, copies in zip(places, pieces):
@@ -250,13 +256,13 @@
     for t in range(1, NJ):
         share = share + zrecv[t]
     mine = own[rows(w * band, band)]
-    for copy in c3:
+    for copy in c2:
         copy.wait_recv()
-    s3 = g3[0]
-    for t in range(1, NQ * NR):
-        s3 = s3 + g3[t]
-    alpha = jnp.sum(s3[:, 0:LANES], axis=1, keepdims=True) / jnp.sum(
-        s3[:, LANES:], axis=1, keepdims=True
+    s2 = g2[0]
+    for t in range(1, NR * NJ):
+        s2 = s2 + g2[t]
+    alpha = jnp.sum(s2[:, 0:LANES], axis=1, keepdims=True) / jnp.sum(
+        s2[:, LANES:], axis=1, keepdims=True
     )
     result[0:band] = share - alpha * mine
     result[band:band + 8] = jnp.broadcast_to(alpha, (8, size))
@@ -275,15 +281,16 @@
     band = size // (NX * NJ)
     block = band * NJ
     hbm = pl.BlockSpec(memory_space=pl.ANY)
-    smem = pl.BlockSpec(memory_space=pltpu.SMEM)
     vmem = pl.BlockSpec(memory_space=pltpu.VMEM)
     full = (size, size)
     result = pl.pallas_call(
         kernel,
         out_shape=jax.ShapeDtypeStruct((band + 8, size), F32),
-        in_specs=[hbm, hbm, hbm, smem, smem, smem],
+        in_specs=[hbm] * 6 + [pl.BlockSpec(memory_space=pltpu.SMEM)],
         out_specs=vmem,
         scratch_shapes=[
+            pltpu.SMEM(left_sizes.shape, jnp.int32),
+            pltpu.SMEM(right_sizes.shape, jnp.int32),
             pltpu.VMEM(full, F32),
             pltpu.VMEM(full, F32),
             pltpu.VMEM(full, F32),
@@ -301,17 +308,17 @@
             pltpu.VMEM((NX - 1, block, size), F32),
             pltpu.VMEM((block, size), F32),
             pltpu.VMEM((NJ, band, size), F32),
-            pltpu.VMEM((NJ, 1, 2 * LANES), F32),
-            pltpu.VMEM((NX * NC, 1, 2 * LANES), F32),
-            pltpu.VMEM((NQ * NR, 1, 2 * LANES), F32),
-            pltpu.SemaphoreType.DMA((3,)),
+            pltpu.VMEM((NX * NQ * NC, 1, 2 * LANES), F32),
+            pltpu.VMEM((NR * NJ, 1, 2 * LANES), F32),
+            pltpu.SemaphoreType.DMA((5,)),
             pltpu.SemaphoreType.DMA((COPIES,)),
             pltpu.SemaphoreType.DMA((COPIES,)),
+            pltpu.SemaphoreType.REGULAR,
         ],
         compiler_params=pltpu.CompilerParams(
             collective_id=0, has_side_effects=True, vmem_limit_bytes=60 << 20
         ),
-    )(state[0], left_env[0, 0], right_env[0, 0], left_sizes, right_sizes, channel_charge)
+    )(state[0], state[0].reshape(2, 4, size // NJ, size), left_env[0, 0], right_env[0, 0], left_sizes, right_sizes, channel_charge)
     share, alpha = pl.pallas_call(
         finish,
         out_shape=(

time: 86 us -> 80.5 us (0.936)
  Pallas kernels: 84 us -> 79 us
    pallas_call x1, Pallas kernels: 82.6 us -> 77.5 us  [per_device(): pl.pallas_call(kernel, out_shape=jax.ShapeDtypeStruct((band + 8, size), F...]
where the time goes in v3:
time: 80.5 us; the launch traced here: 80.2 us
  Pallas kernels  79 us (98%)
  between operations  1.29 us (2%)
    pallas_call x1, Pallas kernels, per_device(): pl.pallas_call(kernel, out_shape=jax.ShapeDtypeStruct((band + 8, size), F...  77.5 us

profile of v3, /device:TPU:1, one launch (start us, length us, event | category | flops | bytes accessed | tf_op | source)
XLA Modules:
  0.0 80.2 jit_solution(900190547681241001)
XLA Ops:
  1.3 77.5 %shard_map.77.result = f32[24,512]{1,0:T(8,128)} custom-call(f32[512,512]{1,0:T(8,128)} %bitcast.6, f32[2,4,64,512]{3,2,1,0:T(8,128)} %bitcast.7, f32[512,512]{1,0:T(8,128)} %bitcast.8, f32[512,512]{1,0:T(8,128)} %bitcast.9, s32[32]{0:T(128)} %lsizes_in.1, s32[32]{0:T(128)} %rsizes_in.1, s32[1]{0:T(128)S(6)} %copy.8.charge), custom_call_target="tpu_custom_call" | custom-call | tf_op jit(solution)/shard_map/pallas_call | solution.py:286
  78.8 1.4 %shard_map.78 = (f32[16,512]{1,0:T(8,128)}, f32[1,1]{1,0:T(1,128)}) custom-call(f32[24,512]{1,0:T(8,128)} %shard_map.77.result), custom_call_target="tpu_custom_call" | custom-call | tf_op jit(solution)/shard_map/pallas_call | solution.py:322

commit v4 on v3

--- a/solution.py
+++ b/solution.py
@@ -36,7 +36,7 @@
     lsizes, rsizes,
     own, lenv, renv, near, far, lh, ll, rh, rl, ph, plo, ih, il, term,
     from_x, zsum, zrecv, g1, g2,
-    local_sem, send_sem, recv_sem, met,
+    local_sem, send_sem, recv_sem, met, told,
 ):
     size = own.shape[0]
     band = size // (NX * NJ)
@@ -63,6 +63,9 @@
     def at_z(step):
         to = lax.rem(r * NJ + j + step, NR * NJ)
         return (x * NJ + to % NJ, (q * NR + to // NJ) * NC + c)
+
+    def at_y(step, core):
+        return (w, (lax.rem(q + step, NQ) * NR + r) * NC + core)
 
     def at_run(step, core):
         return (w, (q * NR + lax.rem(r + step, NR)) * NC + core)
@@ -195,6 +198,10 @@
     x1, x2, x3 = lax.rem(x + 1, NX), lax.rem(x + 2, NX), lax.rem(x + 3, NX)
     nearby.wait_recv()
     inner(x)
+    pl.semaphore_wait(met, 1)
+    tell = [sibling] + [at_y(s, core) for s in (1, NQ - 1) for core in range(NC)]
+    for partner in tell:
+        pl.semaphore_signal(told, inc=1, device_id=partner, device_id_type=MESH)
     for s, xb in ((1, x3), (3, x1), (2, x2)):
         for copies in sent:
             copies[s - 1].wait_recv()
@@ -208,10 +215,11 @@
         term[at] = t
         num = num + lanes(t * own[at])
 
-    pl.semaphore_wait(met, 1)
-    xyc = (x * NQ + q) * NC + c
-    g1[xyc] = jnp.concatenate([num, den], axis=1)
-    c1 = [push(g1.at[xyc], g1.at[xyc], at_xyc(s)) for s in range(1, NX * NQ * NC)]
+    pl.semaphore_wait(told, len(tell))
+    zz = r * NJ + j
+    g2[zz] = jnp.concatenate([num, den], axis=1)
+    farthest_first = sorted(range(1, NR * NJ), key=lambda s: -min(s, NR * NJ - s))
+    c1 = [push(g2.at[zz], g2.at[zz], at_z(s)) for s in farthest_first]
 
     u = j // 2
     places = [3 - u, u + 2 - 4 * (u // 2), u + 1 - 2 * (u % 2), u]
@@ -225,30 +233,32 @@
             for s, xb in ((2, x2), (1, x1), (3, x3))
         ]
 
-    pieces = [scatter(place) for place in places[:2]]
+    pieces = [scatter(place) for place in places]
+    zs = []
+
+    def along_z(some):
+        for place, copies in zip(places[some], pieces[some]):
+            for copy in copies:
+                copy.wait_recv()
+            at = rows(place * pair, pair)
+            zsum[at] = (term[rows(x * block + place * pair, pair)] + from_x[0, at]) + (
+                from_x[1, at] + from_x[2, at]
+            )
+            odd = j % 2
+            two = (2 * place + odd, 2 * place + 1 - odd) if place is not u else (j + 1 - 2 * odd,)
+            for other in two:
+                zs.append(push(zsum.at[rows(other * band, band)], zrecv.at[j], at_j(other)))
+
+    along_z(slice(0, 3))
     for copy in c1:
         copy.wait_recv()
-    zz = r * NJ + j
-    s1 = g1[0]
-    for t in range(1, NX * NQ * NC):
-        s1 = s1 + g1[t]
-    g2[zz] = s1
-    farthest_first = sorted(range(1, NR * NJ), key=lambda s: -min(s, NR * NJ - s))
-    c2 = [push(g2.at[zz], g2.at[zz], at_z(s)) for s in farthest_first]
-    pieces += [scatter(place) for place in places[2:]]
-
-    zs = []
-    for place, copies in zip(places, pieces):
-        for copy in copies:
-            copy.wait_recv()
-        at = rows(place * pair, pair)
-        zsum[at] = (term[rows(x * block + place * pair, pair)] + from_x[0, at]) + (
-            from_x[1, at] + from_x[2, at]
-        )
-        odd = j % 2
-        two = (2 * place + odd, 2 * place + 1 - odd) if place is not u else (j + 1 - 2 * odd,)
-        for other in two:
-            zs.append(push(zsum.at[rows(other * band, band)], zrecv.at[j], at_j(other)))
+    xyc = (x * NQ + q) * NC + c
+    s1 = g2[0]
+    for t in range(1, NR * NJ):
+        s1 = s1 + g2[t]
+    g1[xyc] = s1
+    c2 = [push(g1.at[xyc], g1.at[xyc], at_xyc(s)) for s in range(1, NX * NQ * NC)]
+    along_z(slice(3, 4))
     zrecv[j] = zsum[rows(j * band, band)]
     for copy in zs:
         copy.wait_recv()
@@ -258,9 +268,9 @@
     mine = own[rows(w * band, band)]
     for copy in c2:
         copy.wait_recv()
-    s2 = g2[0]
-    for t in range(1, NR * NJ):
-        s2 = s2 + g2[t]
+    s2 = g1[0]
+    for t in range(1, NX * NQ * NC):
+        s2 = s2 + g1[t]
     alpha = jnp.sum(s2[:, 0:LANES], axis=1, keepdims=True) / jnp.sum(
         s2[:, LANES:], axis=1, keepdims=True
     )
@@ -313,6 +323,7 @@
             pltpu.SemaphoreType.DMA((5,)),
             pltpu.SemaphoreType.DMA((COPIES,)),
             pltpu.SemaphoreType.DMA((COPIES,)),
+            pltpu.SemaphoreType.REGULAR,
             pltpu.SemaphoreType.REGULAR,
         ],
         compiler_params=pltpu.CompilerParams(

time: 80.5 us -> 77.3 us (0.960)
  Pallas kernels: 79 us -> 75.8 us
    pallas_call x1, Pallas kernels: 77.5 us -> 74.4 us  [per_device(): pl.pallas_call(kernel, out_shape=jax.ShapeDtypeStruct((band + 8, size), F...]
where the time goes in v4:
time: 77.3 us; the launch traced here: 77.1 us
  Pallas kernels  75.8 us (98%)
  between operations  1.29 us (2%)
    pallas_call x1, Pallas kernels, per_device(): pl.pallas_call(kernel, out_shape=jax.ShapeDtypeStruct((band + 8, size), F...  74.4 us

profile of v4, /device:TPU:1, one launch (start us, length us, event | category | flops | bytes accessed | tf_op | source)
XLA Modules:
  0.0 77.1 jit_solution(7043919209845813829)
XLA Ops:
  1.3 74.4 %shard_map.77.result = f32[24,512]{1,0:T(8,128)} custom-call(f32[512,512]{1,0:T(8,128)} %bitcast.6, f32[2,4,64,512]{3,2,1,0:T(8,128)} %bitcast.7, f32[512,512]{1,0:T(8,128)} %bitcast.8, f32[512,512]{1,0:T(8,128)} %bitcast.9, s32[32]{0:T(128)} %lsizes_in.1, s32[32]{0:T(128)} %rsizes_in.1, s32[1]{0:T(128)S(6)} %copy.8.charge), custom_call_target="tpu_custom_call" | custom-call | tf_op jit(solution)/shard_map/pallas_call | solution.py:296
  75.7 1.4 %shard_map.78 = (f32[16,512]{1,0:T(8,128)}, f32[1,1]{1,0:T(1,128)}) custom-call(f32[24,512]{1,0:T(8,128)} %shard_map.77.result), custom_call_target="tpu_custom_call" | custom-call | tf_op jit(solution)/shard_map/pallas_call | solution.py:333

commit v5 on v4

--- a/solution.py
+++ b/solution.py
@@ -17,7 +17,7 @@
 NR = 4
 NC = 2
 LANES = 128
-COPIES = 114
+COPIES = 119
 
 
 def split(v):
@@ -169,19 +169,40 @@
     toward = shift * (1 - 2 * c)
 
     def along(src):
-        return [push(src, src, at_x(s)) for s in range(1, NX)]
-
-    quads, sent = [], []
+        return [push(src, src, at_x(s)) for s in (1, 3, 2)]
+
+    def beside(src):
+        return [push(src, src, at_x(s)) for s in (1, 3)]
+
+    def band_of(side, k, t, xb):
+        return far.at[side, k, rows(t * (tall // 2), tall // 2), cols(xb)]
+
+    def relay(k, t, copies):
+        copies[0].wait_recv()
+        onward = band_of(0, k, t, x3)
+        copies.append(push(onward, onward, at_x(1)))
+        copies[1].wait_recv()
+        onward = band_of(1, k, t, x1)
+        copies.append(push(onward, onward, at_x(3)))
+
+    x1, x2, x3 = lax.rem(x + 1, NX), lax.rem(x + 2, NX), lax.rem(x + 3, NX)
+    quads, early, late = [], [], []
     for t in range(2):
         cross[t].wait_recv()
         mine = bands(far, i, t)
         quads.append([push(mine, mine, at_j(h * 4 + to)) for to in quad])
-        sent.append(along(mine))
-    for t in range(2):
-        for copy, to in zip(quads[t], quad):
-            copy.wait_recv()
-            sent.append(along(bands(far, to, t)))
+        early.append((i, t, beside(mine)))
+    for copy, to in zip(quads[0], quad):
+        copy.wait_recv()
+        early.append((to, 0, beside(bands(far, to, 0))))
+    for piece in early[:2]:
+        relay(*piece)
+    for copy, to in zip(quads[1], quad):
+        copy.wait_recv()
+        late.append(along(bands(far, to, 1)))
     pl.semaphore_signal(met, inc=1, device_id=at_j((1 - h) * 4 + i), device_id_type=MESH)
+    for piece in early[2:]:
+        relay(*piece)
 
     def inner(xb):
         at = cols(xb)
@@ -195,16 +216,19 @@
             ph[down], plo[down] = split(took)
         ih[:, at], il[:, at] = split(product(lh[...], ll[...], ph[...], plo[...]))
 
-    x1, x2, x3 = lax.rem(x + 1, NX), lax.rem(x + 2, NX), lax.rem(x + 3, NX)
     nearby.wait_recv()
     inner(x)
     pl.semaphore_wait(met, 1)
     tell = [sibling] + [at_y(s, core) for s in (1, NQ - 1) for core in range(NC)]
     for partner in tell:
         pl.semaphore_signal(told, inc=1, device_id=partner, device_id_type=MESH)
-    for s, xb in ((1, x3), (3, x1), (2, x2)):
-        for copies in sent:
-            copies[s - 1].wait_recv()
+    for place, xb in enumerate((x3, x1, x2)):
+        for copies in late:
+            copies[place].wait_recv()
+        if xb is x2:
+            for _, _, copies in early:
+                copies[2].wait_recv()
+                copies[3].wait_recv()
         inner(xb)
 
     num = jnp.zeros((1, LANES), F32)

time: 77.3 us -> 76.3 us (0.987)
  Pallas kernels: 75.8 us -> 74.8 us
    pallas_call x1, Pallas kernels: 74.4 us -> 73.4 us  [per_device(): pl.pallas_call(kernel, out_shape=jax.ShapeDtypeStruct((band + 8, size), F...]
where the time goes in v5:
time: 76.3 us; the launch traced here: 76.1 us
  Pallas kernels  74.8 us (98%)
  between operations  1.29 us (2%)
    pallas_call x1, Pallas kernels, per_device(): pl.pallas_call(kernel, out_shape=jax.ShapeDtypeStruct((band + 8, size), F...  73.4 us

profile of v5, /device:TPU:1, one launch (start us, length us, event | category | flops | bytes accessed | tf_op | source)
XLA Modules:
  0.0 76.1 jit_solution(18354593931374128568)
XLA Ops:
  1.3 73.4 %shard_map.77.result = f32[24,512]{1,0:T(8,128)} custom-call(f32[512,512]{1,0:T(8,128)} %bitcast.6, f32[2,4,64,512]{3,2,1,0:T(8,128)} %bitcast.7, f32[512,512]{1,0:T(8,128)} %bitcast.8, f32[512,512]{1,0:T(8,128)} %bitcast.9, s32[32]{0:T(128)} %lsizes_in.1, s32[32]{0:T(128)} %rsizes_in.1, s32[1]{0:T(128)S(6)} %copy.8.charge), custom_call_target="tpu_custom_call" | custom-call | tf_op jit(solution)/shard_map/pallas_call | solution.py:320
  74.7 1.4 %shard_map.78 = (f32[16,512]{1,0:T(8,128)}, f32[1,1]{1,0:T(1,128)}) custom-call(f32[24,512]{1,0:T(8,128)} %shard_map.77.result), custom_call_target="tpu_custom_call" | custom-call | tf_op jit(solution)/shard_map/pallas_call | solution.py:357
